TPU v7x, 32 devices: a whole 2x2x4 slice. The times are simulated.
32 devices in a mesh: section: 4 (over x, core), tp: 8 (over z, y).
Axes of the slice: x: 2, y: 2, z: 4, core: 2. Of those that a mesh axis runs over, the one named last changes fastest.
Arguments:
- layer_inputs: bfloat16 [8, 512, 4096], P('section', None, 'tp'), may hold values from -6 to 6
- weights: bfloat16 [8, 4096, 4096], P('section', 'tp'), may hold values from -0.046875 to 0.046875
- input_basis: bfloat16 [8, 4096, 64], P('section', 'tp'), may hold values from -0.09375 to 0.09375
- output_basis: bfloat16 [8, 4096, 32], P('section', 'tp'), may hold values from -0.09375 to 0.09375
- queries: bfloat16 [8, 512, 2048], P('section', 'tp'), may hold values from -0.00390625 to 0.00390625
- top_cotangent: bfloat16 [512, 4096], replicated, may hold values from -6 to 6
- sequence_example: int32 [4], replicated, may hold values from 0 to 1
Outputs:
- scores: float32 [2, 512], P(None, 'tp')
All inputs are finite; a program needn't handle non-finite values.
Results may differ from a plain program's by a relative error of at most 0.0094.
Values may be sent and summed in bfloat16 or wider, within the bound.
A program may use at most 64 MiB of HBM per device.

v0:
```python
import jax
import jax.numpy as jnp
from jax import lax
from jax.sharding import PartitionSpec as P

SEQLEN = 128
SEQ_MB = 1
MB = 4
EXAMPLES = 2


def from_behind(value, axis, by):
    size = lax.axis_size(axis)
    pairs = [(i, i + by) for i in range(size) if 0 <= i + by < size]
    return lax.ppermute(value, axis, pairs)


def silu_parts(values):
    floats = values.astype(jnp.float32)
    logistic = jax.nn.sigmoid(floats)
    return ((floats * logistic).astype(jnp.bfloat16), logistic * (1.0 + floats * (1.0 - logistic)))


def contract_columns(portion, matrix):
    return lax.dot_general(
        portion, matrix, (((1,), (1,)), ((), ())), preferred_element_type=jnp.float32
    )


def outer_rows(out_feats, in_feats):
    joined = out_feats[:, :, :, None] * in_feats[:, :, None, :]
    return joined.reshape(joined.shape[0], joined.shape[1], -1)


def shards(
    layer_inputs, weights, input_basis, output_basis, queries, top_cotangent, sequence_example
):
    section_count = lax.axis_size("section")
    section_rank = lax.axis_index("section")
    tp_rank = lax.axis_index("tp")
    width_local = layer_inputs.shape[2]
    total_tokens = layer_inputs.shape[1]
    block_rows = SEQ_MB * SEQLEN
    activated, slopes = silu_parts(layer_inputs)
    partial_in = jnp.einsum(
        "ltd,ldr->tlr", activated, input_basis, preferred_element_type=jnp.float32
    )
    in_feats = lax.psum(partial_in.reshape(total_tokens, -1), "tp").reshape(partial_in.shape)
    example_index = jnp.arange(EXAMPLES, dtype=jnp.int32)
    is_top = section_rank == section_count - 1

    def fold_upper(portion):
        return contract_columns(portion, weights[1])

    def fold_lower(portion):
        return contract_columns(portion, weights[0])

    def tick(tick_index, state):
        outgoing, grads, stored = state
        micro_index = tick_index - (section_count - 1 - section_rank)
        valid = (micro_index >= 0) & (micro_index < MB)
        micro_clip = jnp.clip(micro_index, 0, MB - 1)
        first_row = micro_clip * block_rows
        slope_block = lax.dynamic_slice_in_dim(slopes, first_row, block_rows, 1)
        received = from_behind(outgoing, "section", -1)
        top_block = lax.dynamic_slice(
            top_cotangent, (first_row, tp_rank * width_local), (block_rows, width_local)
        )
        upper_own = jnp.where(is_top, top_block, received)
        upper_branch = fold_upper(lax.all_gather(upper_own, "tp", axis=1, tiled=True))
        middle_own = (upper_own.astype(jnp.float32) + slope_block[1] * upper_branch).astype(
            jnp.bfloat16
        )
        lower_branch = fold_lower(lax.all_gather(middle_own, "tp", axis=1, tiled=True))
        lower_own = (middle_own.astype(jnp.float32) + slope_block[0] * lower_branch).astype(
            jnp.bfloat16
        )
        cotangents = jnp.stack([middle_own, upper_own], 0)
        partial_out = jnp.einsum(
            "lrd,ldk->rlk", cotangents, output_basis, preferred_element_type=jnp.float32
        )
        out_feats = lax.psum(partial_out.reshape(block_rows, -1), "tp").reshape(partial_out.shape)
        in_block = lax.dynamic_slice_in_dim(in_feats, first_row, block_rows, 0)
        block_examples = jnp.repeat(
            lax.dynamic_slice_in_dim(sequence_example, micro_clip * SEQ_MB, SEQ_MB, 0), SEQLEN
        )
        selector = (example_index[:, None] == block_examples[None, :]).astype(
            jnp.float32
        ) * valid.astype(jnp.float32)
        grads = grads + jnp.einsum(
            "er,rlk->lek",
            selector,
            outer_rows(out_feats, in_block),
            precision=lax.Precision.HIGHEST,
        )
        return (lower_own, grads, stored)

    outgoing_init = jnp.zeros((block_rows, width_local), jnp.bfloat16)
    grads_init = jnp.zeros((2, EXAMPLES, queries.shape[2]), jnp.float32)
    stored_init = jnp.zeros((1,), jnp.bfloat16)
    final_out, grads, stored = lax.fori_loop(
        0, MB + section_count - 1, tick, (outgoing_init, grads_init, stored_init)
    )
    layer_scores = jnp.einsum(
        "lek,lqk->eq", grads, queries.astype(jnp.float32), precision=lax.Precision.HIGHEST
    )
    return lax.psum(layer_scores, "section")


def solution(mesh):
    placed = (
        P("section", None, "tp"),
        P("section", "tp", None),
        P("section", "tp", None),
        P("section", "tp", None),
        P("section", "tp", None),
        P(),
        P(),
    )
    return jax.shard_map(
        shards, mesh=mesh, in_specs=placed, out_specs=P(None, "tp"), check_vma=False
    )
```

profile of v0, /device:TPU:0, one launch (start us, length us, event | category | flops | bytes accessed | tf_op | source)
XLA Modules:
  0.0 749.2 jit_solution(505250659360147819)
XLA Ops:
  6.5 2.7 convolution_bitcast_fusion.2
  9.3 1.9 fusion.28
  11.2 73.2 %all-reduce.2.cloned.1.call-done = f32[512,2,64]{0,2,1:T(8,128)} async-done(((f32[512,2,64]{0,2,1:T(8,128)}), f32[512,2,64]{0,2,1:T(8,128)}) %all-reduce.2.cloned.1.call-update) | async-done | bytes 262160 | tf_op jit(solution)/shard_map/psum | solution.py:48
  84.5 651.5 %while.18 = (s32[]{:T(128)}, bf16[128,512]{1,0:T(8,128)(2,1)S(1)}, f32[2,2,2048]{2,1,0:T(2,128)S(1)}, pred[]{:T(512)}, s32[]{:T(128)}, /*index=5*/bf16[512,4096]...) while((s32[]{:T(128)}, bf16[128,512]{1,0:T(8,128)(2,1)S(1)}, ...), condition=%wide.region_3.4_spmd.clone, body=%wide.region_1.3_spmd.clone.sunk | while | flops 1096048640 | bytes 25756184 | solution.py:101
  85.8 1.9 collective-permute-done
  87.7 1.6 dynamic-slice_select_fusion.2
  89.4 40.3 %all-gather.3.cloned.1.call-done = bf16[128,4096]{1,0:T(8,128)(2,1)} async-done(((bf16[128,512]{1,0:T(8,128)(2,1)}), bf16[128,4096]{1,0:T(8,128)(2,1)}) %all-gather.3.cloned.1.call-update) | async-done | bytes 1048592 | tf_op jit(solution)/shard_map/while/body/eval_jaxpr/all_gather | solution.py:70
  129.7 4.7 add_convert_fusion.4
  137.5 35.6 %psum.31 = f32[128,2,32]{0,2,1:T(8,128)S(1)} all-reduce(f32[128,2,32]{0,2,1:T(8,128)S(1)} %convolution_bitcast_fusion.5), channel_id=1, replica_groups=mesh['section'=4,'tp'=8] {'tp'}, use_global_device_ids=true, to_apply=%region_2.2 | all-reduce | flops 8192 | bytes 65536 | tf_op jit(solution)/shard_map/while/body/eval_jaxpr/psum | solution.py:82
  173.3 1.9 fusion.56
  175.3 4.0 add_convert_fusion.5
  180.7 1.9 collective-permute-done
  184.3 38.2 %all-gather.3.cloned.1.call-done = bf16[128,4096]{1,0:T(8,128)(2,1)} async-done(((bf16[128,512]{1,0:T(8,128)(2,1)}), bf16[128,4096]{1,0:T(8,128)(2,1)}) %all-gather.3.cloned.1.call-update) | async-done | bytes 1048592 | tf_op jit(solution)/shard_map/while/body/eval_jaxpr/all_gather | solution.py:70
  222.5 4.7 add_convert_fusion.4
  230.3 35.6 %psum.31 = f32[128,2,32]{0,2,1:T(8,128)S(1)} all-reduce(f32[128,2,32]{0,2,1:T(8,128)S(1)} %convolution_bitcast_fusion.5), channel_id=1, replica_groups=mesh['section'=4,'tp'=8] {'tp'}, use_global_device_ids=true, to_apply=%region_2.2 | all-reduce | flops 8192 | bytes 65536 | tf_op jit(solution)/shard_map/while/body/eval_jaxpr/psum | solution.py:82
  266.1 1.9 fusion.56
  268.0 4.0 add_convert_fusion.5
  273.5 1.9 collective-permute-done
  277.1 38.2 %all-gather.3.cloned.1.call-done = bf16[128,4096]{1,0:T(8,128)(2,1)} async-done(((bf16[128,512]{1,0:T(8,128)(2,1)}), bf16[128,4096]{1,0:T(8,128)(2,1)}) %all-gather.3.cloned.1.call-update) | async-done | bytes 1048592 | tf_op jit(solution)/shard_map/while/body/eval_jaxpr/all_gather | solution.py:70
  315.3 4.7 add_convert_fusion.4
  323.0 35.6 %psum.31 = f32[128,2,32]{0,2,1:T(8,128)S(1)} all-reduce(f32[128,2,32]{0,2,1:T(8,128)S(1)} %convolution_bitcast_fusion.5), channel_id=1, replica_groups=mesh['section'=4,'tp'=8] {'tp'}, use_global_device_ids=true, to_apply=%region_2.2 | all-reduce | flops 8192 | bytes 65536 | tf_op jit(solution)/shard_map/while/body/eval_jaxpr/psum | solution.py:82
  358.9 1.9 fusion.56
  360.8 4.0 add_convert_fusion.5
  366.3 1.9 collective-permute-done
  369.8 38.2 %all-gather.3.cloned.1.call-done = bf16[128,4096]{1,0:T(8,128)(2,1)} async-done(((bf16[128,512]{1,0:T(8,128)(2,1)}), bf16[128,4096]{1,0:T(8,128)(2,1)}) %all-gather.3.cloned.1.call-update) | async-done | bytes 1048592 | tf_op jit(solution)/shard_map/while/body/eval_jaxpr/all_gather | solution.py:70
  408.0 4.7 add_convert_fusion.4
  415.8 35.6 %psum.31 = f32[128,2,32]{0,2,1:T(8,128)S(1)} all-reduce(f32[128,2,32]{0,2,1:T(8,128)S(1)} %convolution_bitcast_fusion.5), channel_id=1, replica_groups=mesh['section'=4,'tp'=8] {'tp'}, use_global_device_ids=true, to_apply=%region_2.2 | all-reduce | flops 8192 | bytes 65536 | tf_op jit(solution)/shard_map/while/body/eval_jaxpr/psum | solution.py:82
  451.6 1.9 fusion.56
  453.6 4.0 add_convert_fusion.5
  459.0 1.9 collective-permute-done
  462.6 38.2 %all-gather.3.cloned.1.call-done = bf16[128,4096]{1,0:T(8,128)(2,1)} async-done(((bf16[128,512]{1,0:T(8,128)(2,1)}), bf16[128,4096]{1,0:T(8,128)(2,1)}) %all-gather.3.cloned.1.call-update) | async-done | bytes 1048592 | tf_op jit(solution)/shard_map/while/body/eval_jaxpr/all_gather | solution.py:70
  500.8 4.7 add_convert_fusion.4
  508.6 35.6 %psum.31 = f32[128,2,32]{0,2,1:T(8,128)S(1)} all-reduce(f32[128,2,32]{0,2,1:T(8,128)S(1)} %convolution_bitcast_fusion.5), channel_id=1, replica_groups=mesh['section'=4,'tp'=8] {'tp'}, use_global_device_ids=true, to_apply=%region_2.2 | all-reduce | flops 8192 | bytes 65536 | tf_op jit(solution)/shard_map/while/body/eval_jaxpr/psum | solution.py:82
  544.4 1.9 fusion.56
  546.3 4.0 add_convert_fusion.5
  551.8 1.9 collective-permute-done
  555.4 38.2 %all-gather.3.cloned.1.call-done = bf16[128,4096]{1,0:T(8,128)(2,1)} async-done(((bf16[128,512]{1,0:T(8,128)(2,1)}), bf16[128,4096]{1,0:T(8,128)(2,1)}) %all-gather.3.cloned.1.call-update) | async-done | bytes 1048592 | tf_op jit(solution)/shard_map/while/body/eval_jaxpr/all_gather | solution.py:70
  593.6 4.7 add_convert_fusion.4
  601.3 35.6 %psum.31 = f32[128,2,32]{0,2,1:T(8,128)S(1)} all-reduce(f32[128,2,32]{0,2,1:T(8,128)S(1)} %convolution_bitcast_fusion.5), channel_id=1, replica_groups=mesh['section'=4,'tp'=8] {'tp'}, use_global_device_ids=true, to_apply=%region_2.2 | all-reduce | flops 8192 | bytes 65536 | tf_op jit(solution)/shard_map/while/body/eval_jaxpr/psum | solution.py:82
  637.2 1.9 fusion.56
  639.1 4.0 add_convert_fusion.5
  644.6 1.9 collective-permute-done
  648.1 38.2 %all-gather.3.cloned.1.call-done = bf16[128,4096]{1,0:T(8,128)(2,1)} async-done(((bf16[128,512]{1,0:T(8,128)(2,1)}), bf16[128,4096]{1,0:T(8,128)(2,1)}) %all-gather.3.cloned.1.call-update) | async-done | bytes 1048592 | tf_op jit(solution)/shard_map/while/body/eval_jaxpr/all_gather | solution.py:70
  686.3 4.7 add_convert_fusion.4
  694.1 35.6 %psum.31 = f32[128,2,32]{0,2,1:T(8,128)S(1)} all-reduce(f32[128,2,32]{0,2,1:T(8,128)S(1)} %convolution_bitcast_fusion.5), channel_id=1, replica_groups=mesh['section'=4,'tp'=8] {'tp'}, use_global_device_ids=true, to_apply=%region_2.2 | all-reduce | flops 8192 | bytes 65536 | tf_op jit(solution)/shard_map/while/body/eval_jaxpr/psum | solution.py:82
  729.9 1.9 fusion.56
  731.9 4.0 add_convert_fusion.5
  736.4 6.2 psum.28
  (129 shorter events, 43.3 us)
Async XLA Ops:
  6.5 729.4 %copy-start = (bf16[2,64,2048]{2,1,0:T(8,128)(2,1)S(1)}, bf16[2,64,2048]{2,1,0:T(8,128)(2,1)}, u32[]{:S(2)}) copy-start(bf16[2,64,2048]{2,1,0:T(8,128)(2,1)} %param.13) | copy-start | bytes 1572868
  6.5 77.9 %all-reduce.2.cloned.1.call-start = ((), (), s32[]{:S(2)}) async-start(), calls=%async_computation | async-start | bytes 524288 | tf_op jit(solution)/shard_map/psum | solution.py:48
  9.2 75.2 %copy-start.3 = (bf16[2,512,32]{1,2,0:T(8,128)(2,1)S(1)}, bf16[2,512,32]{1,2,0:T(8,128)(2,1)}, u32[]{:S(2)}) copy-start(bf16[2,512,32]{1,2,0:T(8,128)(2,1)} %param.12) | copy-start | bytes 196612
  9.2 75.2 %copy-start.4 = (s32[4]{0:T(128)S(1)}, s32[4]{0:T(128)}, u32[]{:S(2)}) copy-start(s32[4]{0:T(128)} %param.15) | copy-start | bytes 52
  84.5 45.3 %all-gather.3.cloned.1.call-start = ((), (), s32[]{:S(2)}) async-start(), calls=%async_computation.1 | async-start | bytes 1179648 | tf_op jit(solution)/shard_map/while/body/eval_jaxpr/all_gather | solution.py:70
  84.5 3.2 collective-permute-start
  89.3 85.9 %all-gather.5.cloned.1.call-start = ((), (), s32[]{:S(2)}) async-start(), calls=%async_computation.2 | async-start | bytes 1179648 | tf_op jit(solution)/shard_map/while/body/eval_jaxpr/all_gather | solution.py:74
  129.7 6.7 copy-start.1
  173.1 2.2 copy-start.2
  179.3 43.2 %all-gather.3.cloned.1.call-start = ((), (), s32[]{:S(2)}) async-start(), calls=%async_computation.1 | async-start | bytes 1179648 | tf_op jit(solution)/shard_map/while/body/eval_jaxpr/all_gather | solution.py:70
  179.4 3.2 collective-permute-start
  184.3 83.7 %all-gather.5.cloned.1.call-start = ((), (), s32[]{:S(2)}) async-start(), calls=%async_computation.2 | async-start | bytes 1179648 | tf_op jit(solution)/shard_map/while/body/eval_jaxpr/all_gather | solution.py:74
  222.5 6.7 copy-start.1
  265.8 2.2 copy-start.2
  272.1 43.2 %all-gather.3.cloned.1.call-start = ((), (), s32[]{:S(2)}) async-start(), calls=%async_computation.1 | async-start | bytes 1179648 | tf_op jit(solution)/shard_map/while/body/eval_jaxpr/all_gather | solution.py:70
  272.2 3.2 collective-permute-start
  277.0 83.7 %all-gather.5.cloned.1.call-start = ((), (), s32[]{:S(2)}) async-start(), calls=%async_computation.2 | async-start | bytes 1179648 | tf_op jit(solution)/shard_map/while/body/eval_jaxpr/all_gather | solution.py:74
  315.3 6.7 copy-start.1
  358.6 2.2 copy-start.2
  364.9 43.2 %all-gather.3.cloned.1.call-start = ((), (), s32[]{:S(2)}) async-start(), calls=%async_computation.1 | async-start | bytes 1179648 | tf_op jit(solution)/shard_map/while/body/eval_jaxpr/all_gather | solution.py:70
  364.9 3.2 collective-permute-start
  369.8 83.7 %all-gather.5.cloned.1.call-start = ((), (), s32[]{:S(2)}) async-start(), calls=%async_computation.2 | async-start | bytes 1179648 | tf_op jit(solution)/shard_map/while/body/eval_jaxpr/all_gather | solution.py:74
  408.0 6.7 copy-start.1
  451.4 2.2 copy-start.2
  457.6 43.2 %all-gather.3.cloned.1.call-start = ((), (), s32[]{:S(2)}) async-start(), calls=%async_computation.1 | async-start | bytes 1179648 | tf_op jit(solution)/shard_map/while/body/eval_jaxpr/all_gather | solution.py:70
  457.7 3.2 collective-permute-start
  462.6 83.7 %all-gather.5.cloned.1.call-start = ((), (), s32[]{:S(2)}) async-start(), calls=%async_computation.2 | async-start | bytes 1179648 | tf_op jit(solution)/shard_map/while/body/eval_jaxpr/all_gather | solution.py:74
  500.8 6.7 copy-start.1
  544.1 2.2 copy-start.2
  550.4 43.2 %all-gather.3.cloned.1.call-start = ((), (), s32[]{:S(2)}) async-start(), calls=%async_computation.1 | async-start | bytes 1179648 | tf_op jit(solution)/shard_map/while/body/eval_jaxpr/all_gather | solution.py:70
  550.5 3.2 collective-permute-start
  555.3 83.7 %all-gather.5.cloned.1.call-start = ((), (), s32[]{:S(2)}) async-start(), calls=%async_computation.2 | async-start | bytes 1179648 | tf_op jit(solution)/shard_map/while/body/eval_jaxpr/all_gather | solution.py:74
  593.6 6.7 copy-start.1
  636.9 2.2 copy-start.2
  643.2 43.2 %all-gather.3.cloned.1.call-start = ((), (), s32[]{:S(2)}) async-start(), calls=%async_computation.1 | async-start | bytes 1179648 | tf_op jit(solution)/shard_map/while/body/eval_jaxpr/all_gather | solution.py:70
  643.2 3.2 collective-permute-start
  648.1 83.7 %all-gather.5.cloned.1.call-start = ((), (), s32[]{:S(2)}) async-start(), calls=%async_computation.2 | async-start | bytes 1179648 | tf_op jit(solution)/shard_map/while/body/eval_jaxpr/all_gather | solution.py:74
  686.3 6.7 copy-start.1
  729.7 2.2 copy-start.2
Sparse Core Ops, SparseCore 0:
  10.7 73.7 all-reduce.1
  89.5 40.2 all-gather.2
  134.6 38.5 all-gather.4
  184.4 38.0 all-gather.2
  227.3 38.5 all-gather.4
  277.2 38.0 all-gather.2
  320.1 38.5 all-gather.4
  369.9 38.0 all-gather.2
  412.9 38.5 all-gather.4
  462.7 38.0 all-gather.2
  505.6 38.5 all-gather.4
  555.5 38.0 all-gather.2
  598.4 38.5 all-gather.4
  648.2 38.0 all-gather.2
  691.2 38.5 all-gather.4
where the time goes:
time: 750 us; the launch traced here: 749 us
  waiting for transfers between devices  356 us (47%)
  blocking collectives  255 us (34%)
  matrix products  85.2 us (11%)
  other arithmetic  18.8 us (3%)
  between operations  13.1 us (2%)
  local copies, waits for them, and re-layouts  9.96 us (1%)
  starting transfers between devices  9.6 us (1%)
    all_gather x7, waiting for transfers between devices, tick(): lax.all_gather(upper_own, 'tp', axis=1, tiled=True)  269 us
    psum x7, blocking collectives, tick(): lax.psum(partial_out.reshape(block_rows, -1), 'tp')  249 us
    psum x1, waiting for transfers between devices, shards(): lax.psum(partial_in.reshape(total_tokens, -1), 'tp')  73.2 us
    dot_general x14, matrix products, contract_columns(): lax.dot_general(portion, matrix, (((1,), (1,)), ((), ())), preferred_elem...  61.2 us
  transfers between devices with their start and end apart: 22, of which 15 were waited for; matrix products, arithmetic and copies ran while one was open for 5% of the time, Pallas kernels for 0%

commit v1 on v0

v1 whole, which is shorter than its diff:
```python
import functools

import jax
import jax.numpy as jnp
from jax import lax
from jax.experimental import pallas as pl
from jax.experimental.pallas import tpu as pltpu
from jax.sharding import PartitionSpec as P

EXAMPLES = 2
MICRO = 8
MESH = pl.DeviceIdType.MESH
NT = (((1,), (1,)), ((), ()))


def grid_of(tp_count):
    ny = 1
    while (2 * ny) * (2 * ny) <= tp_count:
        ny *= 2
    return tp_count // ny, ny


def slope_of(hidden):
    floats = hidden.astype(jnp.float32)
    logistic = jax.nn.sigmoid(floats)
    return logistic * (1.0 + floats * (1.0 - logistic))


def chain_kernel(
    sections, tp_count, top_ref, w_ref, h_ref, ob_ref, po_ref,
    buf_u, buf_m, buf_l, w_v,
    w_sem, recv_u, recv_m, send_m, send_my, relay_u, relay_m, send_l,
):
    nz, ny = grid_of(tp_count)
    sec = lax.axis_index("section")
    tp = lax.axis_index("tp")
    z, y = tp // ny, lax.rem(tp, ny)
    micro, _, rows, width = buf_u.shape
    is_top = sec == sections - 1
    has_lower = sec > 0

    def peer_z(step):
        return lax.rem(z + step, nz) * ny + y

    def peer_y(step):
        return z * ny + lax.rem(y + step, ny)

    def src_at(zstep, ystep):
        return lax.rem(z + zstep, nz) * ny + lax.rem(y + ystep, ny)

    def w_copy(layer):
        return pltpu.make_async_copy(w_ref.at[layer], w_v.at[layer], w_sem.at[layer])

    def top_copy(m, k):
        return pltpu.make_async_copy(
            top_ref.at[pl.ds(pl.multiple_of(m * rows, rows), rows), pl.ds(k * width, width)],
            buf_u.at[m, k], recv_u.at[m, k])

    def remote(src, dst, ssem, rsem, to_sec, to_tp):
        return pltpu.make_async_remote_copy(
            src_ref=src, dst_ref=dst, send_sem=ssem, recv_sem=rsem,
            device_id=(to_sec, to_tp), device_id_type=MESH)

    @pl.when(is_top)
    def _():
        @pl.loop(0, micro)
        def _(m):
            for k in range(tp_count):
                top_copy(m, k).start()

    w_copy(1).start()
    w_copy(0).start()

    barrier = pltpu.get_barrier_semaphore()
    for step in range(1, nz):
        pl.semaphore_signal(barrier, inc=1, device_id=(sec, peer_z(step)), device_id_type=MESH)
    for step in range(1, ny):
        pl.semaphore_signal(barrier, inc=1, device_id=(sec, peer_y(step)), device_id_type=MESH)

    @pl.when(has_lower)
    def _():
        for step in range(nz):
            pl.semaphore_signal(
                barrier, inc=1, device_id=(sec - 1, peer_z(step)), device_id_type=MESH)

    @pl.when(jnp.logical_not(is_top))
    def _():
        for step in range(nz):
            pl.semaphore_signal(
                barrier, inc=1, device_id=(sec + 1, peer_z(step)), device_id_type=MESH)

    linked = has_lower.astype(jnp.int32) + jnp.logical_not(is_top).astype(jnp.int32)
    pl.semaphore_wait(barrier, nz + ny - 2 + nz * linked)

    def relay_u_copy(m, zstep, ystep):
        src = src_at(zstep, 0)
        return remote(buf_u.at[m, src], buf_u.at[m, src], relay_u.at[m, zstep, ystep],
                      recv_u.at[m, src], sec, peer_y(ystep))

    def relay_m_copy(m, zstep, ystep):
        src = src_at(zstep, 0)
        return remote(buf_m.at[m, src], buf_m.at[m, src], relay_m.at[m, zstep, ystep],
                      recv_m.at[m, src], sec, peer_y(ystep))

    def middle_copy(m, zstep):
        return remote(buf_m.at[m, tp], buf_m.at[m, tp], send_m.at[m, zstep],
                      recv_m.at[m, tp], sec, peer_z(zstep))

    def lower_copy(m, zstep):
        return remote(buf_l.at[m], buf_u.at[m, tp], send_l.at[m, zstep],
                      recv_u.at[m, tp], sec - 1, peer_z(zstep))

    def await_u(m, src):
        remote(buf_u.at[m, src], buf_u.at[m, src], send_my, recv_u.at[m, src], sec, tp).wait_recv()

    def await_m(m, src):
        remote(buf_m.at[m, src], buf_m.at[m, src], send_my, recv_m.at[m, src], sec, tp).wait_recv()

    def product(buf, m, layer):
        total = None
        for k in range(tp_count):
            term = lax.dot_general(
                buf[m, k], w_v[layer, :, k * width:(k + 1) * width], NT,
                preferred_element_type=jnp.float32)
            total = term if total is None else total + term
        return total

    def upper(m):
        at = pl.ds(pl.multiple_of(m * rows, rows), rows)
        own = buf_u[m, tp]
        floats = own.astype(jnp.float32)
        middle = (floats + slope_of(h_ref[1, at, :]) * product(buf_u, m, 1)).astype(jnp.bfloat16)
        buf_m[m, tp] = middle

        @pl.when(has_lower)
        def _():
            for step in range(1, nz):
                middle_copy(m, step).start()
            for step in range(1, ny):
                relay_m_copy(m, 0, step).start()

        po_ref[1, at, :] = jnp.dot(own, ob_ref[1], preferred_element_type=jnp.float32)
        po_ref[0, at, :] = jnp.dot(middle, ob_ref[0], preferred_element_type=jnp.float32)

    def lower(m):
        at = pl.ds(pl.multiple_of(m * rows, rows), rows)
        floats = buf_m[m, tp].astype(jnp.float32)
        buf_l[m] = (floats + slope_of(h_ref[0, at, :]) * product(buf_m, m, 0)).astype(jnp.bfloat16)
        for step in range(nz):
            lower_copy(m, step).start()

    @pl.loop(0, micro + 1)
    def _(it):
        @pl.when(jnp.logical_and(it < micro, jnp.logical_not(is_top)))
        def _():
            for zstep in range(nz):
                await_u(it, src_at(zstep, 0))
                for ystep in range(1, ny):
                    relay_u_copy(it, zstep, ystep).start()

        @pl.when(it == 0)
        def _():
            w_copy(1).wait()

        @pl.when(it == 1)
        def _():
            w_copy(0).wait()

        @pl.when(it < micro)
        def _():
            @pl.when(is_top)
            def _():
                for k in range(tp_count):
                    top_copy(it, k).wait()

            @pl.when(jnp.logical_not(is_top))
            def _():
                for zstep in range(nz):
                    for ystep in range(1, ny):
                        await_u(it, src_at(zstep, ystep))

            upper(it)

        @pl.when(jnp.logical_and(it >= 1, has_lower))
        def _():
            m = it - 1
            for zstep in range(1, nz):
                await_m(m, src_at(zstep, 0))
                for ystep in range(1, ny):
                    relay_m_copy(m, zstep, ystep).start()
            for zstep in range(nz):
                for ystep in range(1, ny):
                    await_m(m, src_at(zstep, ystep))
            lower(m)

    @pl.loop(0, micro)
    def _(m):
        @pl.when(jnp.logical_not(is_top))
        def _():
            for zstep in range(nz):
                for ystep in range(1, ny):
                    relay_u_copy(m, zstep, ystep).wait_send()

        @pl.when(has_lower)
        def _():
            for zstep in range(1, nz):
                middle_copy(m, zstep).wait_send()
            for zstep in range(nz):
                for ystep in range(1, ny):
                    relay_m_copy(m, zstep, ystep).wait_send()
                lower_copy(m, zstep).wait_send()


def chain(sections, tp_count, top, weights, hidden, output_basis):
    tokens = top.shape[0]
    width = hidden.shape[2]
    rows = tokens // MICRO
    nz, ny = grid_of(tp_count)
    dma = pltpu.SemaphoreType.DMA
    vmem = pl.BlockSpec(memory_space=pltpu.VMEM)
    hbm = pl.BlockSpec(memory_space=pl.ANY)
    return pl.pallas_call(
        functools.partial(chain_kernel, sections, tp_count),
        out_shape=jax.ShapeDtypeStruct((2, tokens, output_basis.shape[2]), jnp.float32),
        in_specs=[hbm, hbm, vmem, vmem],
        out_specs=vmem,
        scratch_shapes=[
            pltpu.VMEM((MICRO, tp_count, rows, width), jnp.bfloat16),
            pltpu.VMEM((MICRO, tp_count, rows, width), jnp.bfloat16),
            pltpu.VMEM((MICRO, rows, width), jnp.bfloat16),
            pltpu.VMEM(weights.shape, jnp.bfloat16),
            dma((2,)),
            dma((MICRO, tp_count)),
            dma((MICRO, tp_count)),
            dma((MICRO, nz)),
            dma,
            dma((MICRO, nz, ny)),
            dma((MICRO, nz, ny)),
            dma((MICRO, nz)),
        ],
        compiler_params=pltpu.CompilerParams(
            collective_id=0, has_side_effects=True, vmem_limit_bytes=56 * 2**20),
    )(top, weights, hidden, output_basis)


def shards(
    layer_inputs, weights, input_basis, output_basis, queries, top_cotangent, sequence_example
):
    sections = lax.axis_size("section")
    tp_count = lax.axis_size("tp")
    tokens = layer_inputs.shape[1]
    floats = layer_inputs.astype(jnp.float32)
    activated = (floats * jax.nn.sigmoid(floats)).astype(jnp.bfloat16)
    partial_in = jnp.einsum(
        "ltd,ldr->ltr", activated, input_basis, preferred_element_type=jnp.float32
    )
    in_feats = lax.psum(partial_in, "tp")
    out_feats = chain(sections, tp_count, top_cotangent, weights, layer_inputs, output_basis)
    token_example = jnp.repeat(sequence_example, tokens // sequence_example.shape[0])
    selector = (
        jnp.arange(EXAMPLES, dtype=jnp.int32)[:, None] == token_example[None, :]
    ).astype(jnp.float32)
    chosen = selector[None, :, :, None] * out_feats[:, None]
    partial = jnp.einsum("leto,lti->leoi", chosen, in_feats, precision=lax.Precision.HIGHEST)
    grads = lax.psum(partial.reshape(2, EXAMPLES, -1), "tp")
    layer_scores = jnp.einsum(
        "lek,lqk->eq", grads, queries.astype(jnp.float32), precision=lax.Precision.HIGHEST
    )
    return lax.psum(layer_scores, "section")


def solution(mesh):
    placed = (
        P("section", None, "tp"),
        P("section", "tp", None),
        P("section", "tp", None),
        P("section", "tp", None),
        P("section", "tp", None),
        P(),
        P(),
    )
    return jax.shard_map(
        shards, mesh=mesh, in_specs=placed, out_specs=P(None, "tp"), check_vma=False
    )
```

time: 750 us -> 258 us (0.34)
  waiting for transfers between devices: 356 us -> 0.04 us
  blocking collectives: 255 us -> 43.2 us
  Pallas kernels: 0 us -> 194 us
  matrix products: 85.2 us -> 4.56 us
  other arithmetic: 18.8 us -> 0.01 us
  starting transfers between devices: 9.6 us -> 0.01 us
  local copies, waits for them, and re-layouts: 9.96 us -> 2.24 us
    all_gather x14 -> x0, waiting for transfers between devices: 269 us -> none  [the longest x7 269 us: tick(): lax.all_gather(upper_own, 'tp', axis=1, tiled=True)]
    psum x7 -> x1, blocking collectives: 249 us -> 36.9 us  [shards(): grads = lax.psum(partial.reshape(2, EXAMPLES, -1), 'tp')]
    pallas_call x0 -> x1, Pallas kernels: none -> 194 us  [chain(): pl.pallas_call(functools.partial(chain_kernel, sections, tp_count), out_s...]
    dot_general x29 -> x2, matrix products: 84.7 us -> 4.05 us  [the longest x1 2.71 us: shards(): jnp.einsum('ltd,ldr->ltr', activated, input_basis, preferred_element_type...]
    psum x1, waiting for transfers between devices: 73.2 us -> 0.02 us  [shards(): in_feats = lax.psum(partial_in, 'tp')]
    ppermute x7 -> x0, waiting for transfers between devices: 13.5 us -> none  [from_behind(): return lax.ppermute(value, axis, pairs)]
    select_n x7 -> x0, other arithmetic: 11.1 us -> none  [tick(): upper_own = jnp.where(is_top, top_block, received)]
    dynamic_slice x14 -> x0, local copies, waits for them, and re-layouts: 9.9 us -> none  [the longest x7 5.97 us: tick(): in_block = lax.dynamic_slice_in_dim(in_feats, first_row, block_rows, 0)]
  transfers between devices with their start and end apart: 22 -> 1, of which waited for: 15 -> 0; matrix products, arithmetic and copies ran while one was open for 5% -> 1% of each run, Pallas kernels for 0% -> 75%
where the time goes in v1:
time: 258 us
  Pallas kernels  194 us (75%)
  blocking collectives  43.2 us (17%)
  between operations  13.4 us (5%)
  matrix products  4.56 us (2%)
    pallas_call x1, Pallas kernels, chain(): pl.pallas_call(functools.partial(chain_kernel, sections, tp_count), out_s...  194 us
    psum x1, blocking collectives, shards(): grads = lax.psum(partial.reshape(2, EXAMPLES, -1), 'tp')  36.9 us
    psum x1, blocking collectives, shards(): return lax.psum(layer_scores, 'section')  6.3 us
  transfers between devices with their start and end apart: 1, of which 0 were waited for; matrix products, arithmetic and copies ran while one was open for 1% of the time, Pallas kernels for 75%

profile of v1, /device:TPU:0, one launch (start us, length us, event | category | flops | bytes accessed | tf_op | source)
XLA Modules:
  0.0 257.5 jit_solution(919447666825347013)
XLA Ops:
  6.5 0.0 copy-start
  6.5 0.0 copy-start.2
  6.5 0.0 copy-start.1
  6.5 0.0 all-reduce.2.cloned.1.call-start
  6.5 2.7 %fusion.4 = f32[2,512,64]{1,2,0:T(8,128)} fusion(bf16[2,512,64]{1,2,0:T(8,128)(2,1)} %param.9, bf16[2,512,512]{2,1,0:T(8,128)(2,1)} %h_ref.1), kind=kOutput, calls=%fused_computation.7 | convolution fusion | flops 70254592 | bytes 1441792 | tf_op jit(solution)/shard_map/ltd,ldr->ltr/dot_general | solution.py:254
  9.3 0.0 all-reduce.2.cloned.1.call-update
  9.3 0.0 copy-done.2
  9.3 0.1 broadcast_bitcast_fusion
  9.4 0.0 copy-done.1
  9.4 0.9 copy.8.ob_ref
  10.2 194.1 %shard_map.73 = f32[2,512,32]{2,1,0:T(8,128)} custom-call(bf16[512,4096]{1,0:T(8,128)(2,1)} %top_ref.1, bf16[2,512,4096]{2,1,0:T(8,128)(2,1)} %w_ref.1, bf16[2,512,512]{2,1,0:T(8,128)(2,1)} %h_ref.1, bf16[2,512,32]{2,1,0:T(8,128)(2,1)} %copy.8.ob_ref), custom_call_target="tpu_custom_call" | custom-call | tf_op jit(solution)/shard_map/pallas_call | solution.py:222
  204.3 1.2 copy.9
  205.5 0.0 all-reduce.2.cloned.1.call-done
  205.6 1.3 fusion.6
  206.9 0.1 reshape.29
  207.0 36.9 %psum.22 = f32[2,2,2048]{2,1,0:T(2,128)S(1)} all-reduce(f32[2,2,2048]{2,1,0:T(2,128)S(1)} %reshape.29), channel_id=1, replica_groups=mesh['section'=4,'tp'=8] {'tp'}, use_global_device_ids=true, to_apply=%region_1.0 | all-reduce | flops 8192 | bytes 65536 | tf_op jit(solution)/shard_map/psum | solution.py:265
  243.9 0.0 copy-done
  243.9 0.5 convolution_bitcast_fusion
  244.4 6.3 %psum.23 = f32[2,64]{1,0:T(2,128)} all-reduce(f32[2,64]{1,0:T(2,128)S(1)} %convolution_bitcast_fusion), channel_id=1, replica_groups=mesh['section'=4,'tp'=8] {'section'}, use_global_device_ids=true, to_apply=%region_2.0 | all-reduce | flops 128 | bytes 1024 | tf_op jit(solution)/shard_map/psum | solution.py:269
  (1 shorter events, 0.0 us)
Async XLA Ops:
  6.5 237.3 %copy-start = (bf16[2,64,2048]{2,1,0:T(8,128)(2,1)S(1)}, bf16[2,64,2048]{2,1,0:T(8,128)(2,1)}, u32[]{:S(2)}) copy-start(bf16[2,64,2048]{2,1,0:T(8,128)(2,1)} %param.11) | copy-start | bytes 1572868
  6.5 2.7 %copy-start.2 = (s32[4]{0:T(128)S(1)}, s32[4]{0:T(128)}, u32[]{:S(2)}) copy-start(s32[4]{0:T(128)} %param.13) | copy-start | bytes 52
  6.5 2.8 %copy-start.1 = (bf16[2,512,32]{1,2,0:T(8,128)(2,1)S(1)}, bf16[2,512,32]{1,2,0:T(8,128)(2,1)}, u32[]{:S(2)}) copy-start(bf16[2,512,32]{1,2,0:T(8,128)(2,1)} %param.10) | copy-start | bytes 196612
  6.5 199.0 %all-reduce.2.cloned.1.call-start = ((), (), s32[]{:S(2)}) async-start(), calls=%async_computation | async-start | bytes 524288 | tf_op jit(solution)/shard_map/psum | solution.py:257
Sparse Core Ops, SparseCore 0:
  10.7 76.2 all-reduce.1

commit v2 on v1

--- a/solution.py
+++ b/solution.py
@@ -8,7 +8,6 @@
 from jax.sharding import PartitionSpec as P
 
 EXAMPLES = 2
-MICRO = 8
 MESH = pl.DeviceIdType.MESH
 NT = (((1,), (1,)), ((), ()))
 
@@ -27,9 +26,10 @@
 
 
 def chain_kernel(
-    sections, tp_count, top_ref, w_ref, h_ref, ob_ref, po_ref,
-    buf_u, buf_m, buf_l, w_v,
+    sections, tp_count, top_ref, w_ref, h_ref, ib_ref, ob_ref, q_ref, se_ref, score_ref,
+    buf_u, buf_m, buf_l, w_v, ob_v, ib_v, out_v, part_in, got_in, full_in, grad_v, sum_v, score_v,
     w_sem, recv_u, recv_m, send_m, send_my, relay_u, relay_m, send_l,
+    part_send, part_recv, full_send, full_recv, grad_send, grad_recv, score_send, score_recv,
 ):
     nz, ny = grid_of(tp_count)
     sec = lax.axis_index("section")
@@ -61,6 +61,19 @@
             src_ref=src, dst_ref=dst, send_sem=ssem, recv_sem=rsem,
             device_id=(to_sec, to_tp), device_id_type=MESH)
 
+    rank_in, rank_out = ib_ref.shape[2], ob_ref.shape[2]
+
+    def prepare_bases():
+        gap_in = jnp.zeros((width, rank_in), jnp.float32)
+        gap_out = jnp.zeros((width, EXAMPLES * rank_out), jnp.float32)
+        for layer in range(2):
+            basis_in = ib_ref[layer].astype(jnp.float32)
+            basis_out = [ob_ref[layer].astype(jnp.float32)] * EXAMPLES
+            ins = [basis_in, gap_in] if layer == 0 else [gap_in, basis_in]
+            outs = basis_out + [gap_out] if layer == 0 else [gap_out] + basis_out
+            ib_v[layer] = jnp.concatenate(ins, 1).astype(jnp.bfloat16)
+            ob_v[layer] = jnp.concatenate(outs, 1).astype(jnp.bfloat16)
+
     @pl.when(is_top)
     def _():
         @pl.loop(0, micro)
@@ -72,25 +85,33 @@
     w_copy(0).start()
 
     barrier = pltpu.get_barrier_semaphore()
-    for step in range(1, nz):
-        pl.semaphore_signal(barrier, inc=1, device_id=(sec, peer_z(step)), device_id_type=MESH)
-    for step in range(1, ny):
-        pl.semaphore_signal(barrier, inc=1, device_id=(sec, peer_y(step)), device_id_type=MESH)
+
+    def greet(to_sec, to_tp):
+        pl.semaphore_signal(barrier, inc=1, device_id=(to_sec, to_tp), device_id_type=MESH)
+
+    for step in range(1, tp_count):
+        greet(sec, lax.rem(tp + step, tp_count))
 
     @pl.when(has_lower)
     def _():
         for step in range(nz):
-            pl.semaphore_signal(
-                barrier, inc=1, device_id=(sec - 1, peer_z(step)), device_id_type=MESH)
+            greet(sec - 1, peer_z(step))
 
     @pl.when(jnp.logical_not(is_top))
     def _():
         for step in range(nz):
-            pl.semaphore_signal(
-                barrier, inc=1, device_id=(sec + 1, peer_z(step)), device_id_type=MESH)
-
+            greet(sec + 1, peer_z(step))
+
+    for step in range(1, sections):
+        other = lax.rem(sec + step, sections)
+
+        @pl.when(jnp.logical_and(other != sec + 1, other != sec - 1))
+        def _(other=other):
+            greet(other, tp)
+
+    prepare_bases()
     linked = has_lower.astype(jnp.int32) + jnp.logical_not(is_top).astype(jnp.int32)
-    pl.semaphore_wait(barrier, nz + ny - 2 + nz * linked)
+    pl.semaphore_wait(barrier, tp_count + sections - 2 + (nz - 1) * linked)
 
     def relay_u_copy(m, zstep, ystep):
         src = src_at(zstep, 0)
@@ -139,8 +160,12 @@
             for step in range(1, ny):
                 relay_m_copy(m, 0, step).start()
 
-        po_ref[1, at, :] = jnp.dot(own, ob_ref[1], preferred_element_type=jnp.float32)
-        po_ref[0, at, :] = jnp.dot(middle, ob_ref[0], preferred_element_type=jnp.float32)
+        feats = jnp.dot(own, ob_v[1], preferred_element_type=jnp.float32) + jnp.dot(
+            middle, ob_v[0], preferred_element_type=jnp.float32)
+        example = se_ref[m * rows // (micro * rows // se_ref.shape[0])]
+        lane_example = lax.rem(
+            lax.broadcasted_iota(jnp.int32, feats.shape, 1) // rank_out, EXAMPLES)
+        out_v[at, :] = jnp.where(lane_example == example, feats, 0.0)
 
     def lower(m):
         at = pl.ds(pl.multiple_of(m * rows, rows), rows)
@@ -149,14 +174,73 @@
         for step in range(nz):
             lower_copy(m, step).start()
 
+    def tp_copy(src, dst, ssem, rsem, to_tp):
+        return remote(src, dst, ssem, rsem, sec, to_tp)
+
+    def part_copy(step):
+        to = lax.rem(tp + step, tp_count)
+        return tp_copy(part_in.at[to], got_in.at[tp], part_send.at[step], part_recv.at[tp], to)
+
+    def full_copy(step):
+        to = lax.rem(tp + step, tp_count)
+        return tp_copy(full_in.at[tp], full_in.at[tp], full_send.at[step], full_recv.at[tp], to)
+
+    def grad_copy(step):
+        to = lax.rem(tp + step, tp_count)
+        return tp_copy(grad_v.at[tp], grad_v.at[tp], grad_send.at[step], grad_recv.at[tp], to)
+
+    def score_copy(step):
+        to = lax.rem(sec + step, sections)
+        return remote(score_v.at[sec], score_v.at[sec], score_send.at[step],
+                      score_recv.at[sec], to, tp)
+
+    def project_inputs():
+        @pl.loop(0, tp_count)
+        def _(k):
+            at = pl.ds(pl.multiple_of(k * rows, rows), rows)
+            total = None
+            for layer in range(2):
+                floats = h_ref[layer, at, :].astype(jnp.float32)
+                activated = (floats * jax.nn.sigmoid(floats)).astype(jnp.bfloat16)
+                term = jnp.dot(activated, ib_v[layer], preferred_element_type=jnp.float32)
+                total = term if total is None else total + term
+            part_in[k] = total
+
+        for step in range(1, tp_count):
+            part_copy(step).start()
+        total = part_in[tp]
+        for step in range(1, tp_count):
+            src = lax.rem(tp + step, tp_count)
+            tp_copy(got_in.at[src], got_in.at[src], send_my, part_recv.at[src], tp).wait_recv()
+            total = total + got_in[src]
+        full_in[tp] = total
+        for step in range(1, tp_count):
+            full_copy(step).start()
+
+    @pl.when(jnp.logical_not(is_top))
+    def _():
+        project_inputs()
+
+    def pass_middle(m):
+        for zstep in range(1, nz):
+            await_m(m, src_at(zstep, 0))
+            for ystep in range(1, ny):
+                relay_m_copy(m, zstep, ystep).start()
+
     @pl.loop(0, micro + 1)
     def _(it):
+        with_middle = jnp.logical_and(it >= 1, has_lower)
+
         @pl.when(jnp.logical_and(it < micro, jnp.logical_not(is_top)))
         def _():
             for zstep in range(nz):
                 await_u(it, src_at(zstep, 0))
                 for ystep in range(1, ny):
                     relay_u_copy(it, zstep, ystep).start()
+
+        @pl.when(jnp.logical_and(with_middle, jnp.logical_not(is_top)))
+        def _():
+            pass_middle(it - 1)
 
         @pl.when(it == 0)
         def _():
@@ -181,17 +265,76 @@
 
             upper(it)
 
-        @pl.when(jnp.logical_and(it >= 1, has_lower))
+        @pl.when(with_middle)
         def _():
             m = it - 1
-            for zstep in range(1, nz):
-                await_m(m, src_at(zstep, 0))
-                for ystep in range(1, ny):
-                    relay_m_copy(m, zstep, ystep).start()
+
+            @pl.when(is_top)
+            def _():
+                pass_middle(m)
+
             for zstep in range(nz):
                 for ystep in range(1, ny):
                     await_m(m, src_at(zstep, ystep))
             lower(m)
+
+    @pl.when(is_top)
+    def _():
+        project_inputs()
+
+    for step in range(1, tp_count):
+        src = lax.rem(tp + step, tp_count)
+        tp_copy(full_in.at[src], full_in.at[src], send_my, full_recv.at[src], tp).wait_recv()
+    lanes = 2 * rank_in
+    pairs = EXAMPLES * rank_out
+    product_all = lax.dot_general(
+        out_v[...], full_in[...].reshape(micro * rows, lanes), (((0,), (0,)), ((), ())),
+        precision=lax.Precision.HIGHEST, preferred_element_type=jnp.float32)
+    lane = lax.broadcasted_iota(jnp.int32, (pairs, lanes), 1)
+    grad_v[tp] = jnp.where(lane < rank_in, product_all[:pairs], product_all[pairs:])
+    for step in range(1, tp_count):
+        grad_copy(step).start()
+    for step in range(1, tp_count):
+        src = lax.rem(tp + step, tp_count)
+        tp_copy(grad_v.at[src], grad_v.at[src], send_my, grad_recv.at[src], tp).wait_recv()
+    total = grad_v[0]
+    for k in range(1, tp_count):
+        total = total + grad_v[k]
+    sum_v[...] = total
+    half = rank_out // 2
+    number = q_ref.shape[1]
+    sums = []
+    for example in range(EXAMPLES):
+        even = sum_v[pl.ds(example * rank_out, half, stride=2), :]
+        odd = sum_v[pl.ds(example * rank_out + 1, half, stride=2), :]
+        acc = jnp.zeros((number, lanes), jnp.float32)
+        for layer in range(2):
+            part = slice(layer * rank_in, (layer + 1) * rank_in)
+            tiles = jnp.concatenate([even[:, part], odd[:, part]], 1)
+            for j in range(half):
+                block = q_ref[layer, :, j * lanes:(j + 1) * lanes].astype(jnp.float32)
+                acc = acc + tiles[j:j + 1, :] * block
+        sums.append(acc)
+    score_v[sec] = lax.dot_general(
+        jnp.ones((8, lanes), jnp.float32), jnp.concatenate(sums, 0), NT,
+        precision=lax.Precision.HIGHEST, preferred_element_type=jnp.float32)
+    for step in range(1, sections):
+        score_copy(step).start()
+    for step in range(1, sections):
+        src = lax.rem(sec + step, sections)
+        remote(score_v.at[src], score_v.at[src], send_my, score_recv.at[src], sec, tp).wait_recv()
+    total = score_v[0]
+    for k in range(1, sections):
+        total = total + score_v[k]
+    for example in range(EXAMPLES):
+        score_ref[example:example + 1, :] = total[0:1, example * number:(example + 1) * number]
+
+    for step in range(1, tp_count):
+        part_copy(step).wait_send()
+        full_copy(step).wait_send()
+        grad_copy(step).wait_send()
+    for step in range(1, sections):
+        score_copy(step).wait_send()
 
     @pl.loop(0, micro)
     def _(m):
@@ -211,62 +354,61 @@
                 lower_copy(m, zstep).wait_send()
 
 
-def chain(sections, tp_count, top, weights, hidden, output_basis):
-    tokens = top.shape[0]
-    width = hidden.shape[2]
-    rows = tokens // MICRO
-    nz, ny = grid_of(tp_count)
-    dma = pltpu.SemaphoreType.DMA
-    vmem = pl.BlockSpec(memory_space=pltpu.VMEM)
-    hbm = pl.BlockSpec(memory_space=pl.ANY)
-    return pl.pallas_call(
-        functools.partial(chain_kernel, sections, tp_count),
-        out_shape=jax.ShapeDtypeStruct((2, tokens, output_basis.shape[2]), jnp.float32),
-        in_specs=[hbm, hbm, vmem, vmem],
-        out_specs=vmem,
-        scratch_shapes=[
-            pltpu.VMEM((MICRO, tp_count, rows, width), jnp.bfloat16),
-            pltpu.VMEM((MICRO, tp_count, rows, width), jnp.bfloat16),
-            pltpu.VMEM((MICRO, rows, width), jnp.bfloat16),
-            pltpu.VMEM(weights.shape, jnp.bfloat16),
-            dma((2,)),
-            dma((MICRO, tp_count)),
-            dma((MICRO, tp_count)),
-            dma((MICRO, nz)),
-            dma,
-            dma((MICRO, nz, ny)),
-            dma((MICRO, nz, ny)),
-            dma((MICRO, nz)),
-        ],
-        compiler_params=pltpu.CompilerParams(
-            collective_id=0, has_side_effects=True, vmem_limit_bytes=56 * 2**20),
-    )(top, weights, hidden, output_basis)
-
-
 def shards(
     layer_inputs, weights, input_basis, output_basis, queries, top_cotangent, sequence_example
 ):
     sections = lax.axis_size("section")
     tp_count = lax.axis_size("tp")
-    tokens = layer_inputs.shape[1]
-    floats = layer_inputs.astype(jnp.float32)
-    activated = (floats * jax.nn.sigmoid(floats)).astype(jnp.bfloat16)
-    partial_in = jnp.einsum(
-        "ltd,ldr->ltr", activated, input_basis, preferred_element_type=jnp.float32
-    )
-    in_feats = lax.psum(partial_in, "tp")
-    out_feats = chain(sections, tp_count, top_cotangent, weights, layer_inputs, output_basis)
-    token_example = jnp.repeat(sequence_example, tokens // sequence_example.shape[0])
-    selector = (
-        jnp.arange(EXAMPLES, dtype=jnp.int32)[:, None] == token_example[None, :]
-    ).astype(jnp.float32)
-    chosen = selector[None, :, :, None] * out_feats[:, None]
-    partial = jnp.einsum("leto,lti->leoi", chosen, in_feats, precision=lax.Precision.HIGHEST)
-    grads = lax.psum(partial.reshape(2, EXAMPLES, -1), "tp")
-    layer_scores = jnp.einsum(
-        "lek,lqk->eq", grads, queries.astype(jnp.float32), precision=lax.Precision.HIGHEST
-    )
-    return lax.psum(layer_scores, "section")
+    tokens, width = layer_inputs.shape[1:]
+    micro = tp_count
+    rows = tokens // micro
+    nz, ny = grid_of(tp_count)
+    lanes = 2 * input_basis.shape[2]
+    pairs = EXAMPLES * output_basis.shape[2]
+    number = queries.shape[1]
+    dma = pltpu.SemaphoreType.DMA
+    vmem = pl.BlockSpec(memory_space=pltpu.VMEM)
+    hbm = pl.BlockSpec(memory_space=pl.ANY)
+    smem = pl.BlockSpec(memory_space=pltpu.SMEM)
+    return pl.pallas_call(
+        functools.partial(chain_kernel, sections, tp_count),
+        out_shape=jax.ShapeDtypeStruct((EXAMPLES, number), jnp.float32),
+        in_specs=[hbm, hbm, vmem, vmem, vmem, vmem, smem],
+        out_specs=vmem,
+        scratch_shapes=[
+            pltpu.VMEM((micro, tp_count, rows, width), jnp.bfloat16),
+            pltpu.VMEM((micro, tp_count, rows, width), jnp.bfloat16),
+            pltpu.VMEM((micro, rows, width), jnp.bfloat16),
+            pltpu.VMEM(weights.shape, jnp.bfloat16),
+            pltpu.VMEM((2, width, 2 * pairs), jnp.bfloat16),
+            pltpu.VMEM((2, width, lanes), jnp.bfloat16),
+            pltpu.VMEM((tokens, 2 * pairs), jnp.float32),
+            pltpu.VMEM((tp_count, rows, lanes), jnp.float32),
+            pltpu.VMEM((tp_count, rows, lanes), jnp.float32),
+            pltpu.VMEM((tp_count, rows, lanes), jnp.float32),
+            pltpu.VMEM((tp_count, pairs, lanes), jnp.float32),
+            pltpu.VMEM((pairs, lanes), jnp.float32),
+            pltpu.VMEM((sections, 8, EXAMPLES * number), jnp.float32),
+            dma((2,)),
+            dma((micro, tp_count)),
+            dma((micro, tp_count)),
+            dma((micro, nz)),
+            dma,
+            dma((micro, nz, ny)),
+            dma((micro, nz, ny)),
+            dma((micro, nz)),
+            dma((tp_count,)),
+            dma((tp_count,)),
+            dma((tp_count,)),
+            dma((tp_count,)),
+            dma((tp_count,)),
+            dma((tp_count,)),
+            dma((sections,)),
+            dma((sections,)),
+        ],
+        compiler_params=pltpu.CompilerParams(
+            collective_id=0, has_side_effects=True, vmem_limit_bytes=56 * 2**20),
+    )(top_cotangent, weights, layer_inputs, input_basis, output_basis, queries, sequence_example)
 
 
 def solution(mesh):

time: 258 us -> 186 us (0.72)
  blocking collectives: 43.2 us -> 0 us
  between operations: 13.4 us -> 0.01 us
  Pallas kernels: 194 us -> 181 us
  matrix products: 4.56 us -> 0 us
    psum x2 -> x0, blocking collectives: 43.2 us -> none  [the longest x1 36.9 us: shards(): grads = lax.psum(partial.reshape(2, EXAMPLES, -1), 'tp')]
    pallas_call x1, Pallas kernels: 194 us -> 181 us  [shards(): pl.pallas_call(functools.partial(chain_kernel, sections, tp_count), out_s...]
    dot_general x3 -> x0, matrix products: 4.56 us -> none  [the longest x1 2.71 us: shards(): jnp.einsum('ltd,ldr->ltr', activated, input_basis, preferred_element_type...]
    unnamed x7 -> x3, local copies, waits for them, and re-layouts: 0.87 us -> 4.65 us
  transfers between devices with their start and end apart: 1 -> 0, of which waited for: 0 -> 0; matrix products, arithmetic and copies ran while one was open for 1% -> 0% of each run, Pallas kernels for 75% -> 0%
where the time goes in v2:
time: 186 us
  Pallas kernels  181 us (97%)
  local copies, waits for them, and re-layouts  4.65 us (3%)
    pallas_call x1, Pallas kernels, shards(): pl.pallas_call(functools.partial(chain_kernel, sections, tp_count), out_s...  181 us
    unnamed x3, local copies, waits for them, and re-layouts  4.65 us

profile of v2, /device:TPU:0, one launch (start us, length us, event | category | flops | bytes accessed | tf_op | source)
XLA Modules:
  0.0 186.1 jit_solution(6519137948198127456)
XLA Ops:
  0.0 1.7 copy.8.ib_ref
  1.7 1.7 copy.9.ob_ref
  3.4 181.5 %shard_map.73 = f32[2,64]{1,0:T(2,128)} custom-call(bf16[512,4096]{1,0:T(8,128)(2,1)} %top_ref.1, bf16[2,512,4096]{2,1,0:T(8,128)(2,1)} %w_ref.1, bf16[2,512,512]{2,1,0:T(8,128)(2,1)} %h_ref.1, bf16[2,512,64]{2,1,0:T(8,128)(2,1)} %copy.8.ib_ref, bf16[2,512,32]{2,1,0:T(8,128)(2,1)} %copy.9.ob_ref, bf16[2,64,2048]{2,1,0:T(8,128)(2,1)} %q_ref.1, s32[4]{0:T(128)} %se_ref.1), custom_call_target="tpu_custom_call" | custom-call | tf_op jit(solution)/shard_map/pallas_call | solution.py:373
  184.9 1.2 copy.11

commit v3 on v2

--- a/solution.py
+++ b/solution.py
@@ -39,14 +39,22 @@
     is_top = sec == sections - 1
     has_lower = sec > 0
 
+    far = [z]
+    for k in range(nz - 1):
+        down = nz - 1 - k
+        from_low = down - (z >= down).astype(jnp.int32)
+        from_high = k + (z <= k).astype(jnp.int32)
+        far.append(jnp.where(z < nz // 2, from_low, from_high))
+    near = far[:1] + far[:0:-1]
+
     def peer_z(step):
-        return lax.rem(z + step, nz) * ny + y
+        return far[step] * ny + y
 
     def peer_y(step):
         return z * ny + lax.rem(y + step, ny)
 
     def src_at(zstep, ystep):
-        return lax.rem(z + zstep, nz) * ny + lax.rem(y + ystep, ny)
+        return near[zstep] * ny + lax.rem(y + ystep, ny)
 
     def w_copy(layer):
         return pltpu.make_async_copy(w_ref.at[layer], w_v.at[layer], w_sem.at[layer])
@@ -61,18 +69,18 @@
             src_ref=src, dst_ref=dst, send_sem=ssem, recv_sem=rsem,
             device_id=(to_sec, to_tp), device_id_type=MESH)
 
-    rank_in, rank_out = ib_ref.shape[2], ob_ref.shape[2]
+    rank_in, rank_out = ib_ref.shape[1], ob_ref.shape[1]
 
     def prepare_bases():
-        gap_in = jnp.zeros((width, rank_in), jnp.float32)
-        gap_out = jnp.zeros((width, EXAMPLES * rank_out), jnp.float32)
+        gap_in = jnp.zeros((rank_in, width), jnp.float32)
+        gap_out = jnp.zeros((EXAMPLES * rank_out, width), jnp.float32)
         for layer in range(2):
             basis_in = ib_ref[layer].astype(jnp.float32)
             basis_out = [ob_ref[layer].astype(jnp.float32)] * EXAMPLES
             ins = [basis_in, gap_in] if layer == 0 else [gap_in, basis_in]
             outs = basis_out + [gap_out] if layer == 0 else [gap_out] + basis_out
-            ib_v[layer] = jnp.concatenate(ins, 1).astype(jnp.bfloat16)
-            ob_v[layer] = jnp.concatenate(outs, 1).astype(jnp.bfloat16)
+            ib_v[layer] = jnp.concatenate(ins, 0).astype(jnp.bfloat16)
+            ob_v[layer] = jnp.concatenate(outs, 0).astype(jnp.bfloat16)
 
     @pl.when(is_top)
     def _():
@@ -137,12 +145,12 @@
     def await_m(m, src):
         remote(buf_m.at[m, src], buf_m.at[m, src], send_my, recv_m.at[m, src], sec, tp).wait_recv()
 
-    def product(buf, m, layer):
-        total = None
-        for k in range(tp_count):
+    def product(buf, m, layer, ystep, total=None):
+        for zstep in range(nz):
+            src = src_at(zstep, ystep)
+            columns = pl.ds(pl.multiple_of(src * width, width), width)
             term = lax.dot_general(
-                buf[m, k], w_v[layer, :, k * width:(k + 1) * width], NT,
-                preferred_element_type=jnp.float32)
+                buf[m, src], w_v[layer, :, columns], NT, preferred_element_type=jnp.float32)
             total = term if total is None else total + term
         return total
 
@@ -150,7 +158,16 @@
         at = pl.ds(pl.multiple_of(m * rows, rows), rows)
         own = buf_u[m, tp]
         floats = own.astype(jnp.float32)
-        middle = (floats + slope_of(h_ref[1, at, :]) * product(buf_u, m, 1)).astype(jnp.bfloat16)
+        slope = slope_of(h_ref[1, at, :])
+        total = product(buf_u, m, 1, 0)
+        for ystep in range(1, ny):
+            @pl.when(jnp.logical_not(is_top))
+            def _(ystep=ystep):
+                for zstep in range(nz):
+                    await_u(m, src_at(zstep, ystep))
+
+            total = product(buf_u, m, 1, ystep, total)
+        middle = (floats + slope * total).astype(jnp.bfloat16)
         buf_m[m, tp] = middle
 
         @pl.when(has_lower)
@@ -160,8 +177,9 @@
             for step in range(1, ny):
                 relay_m_copy(m, 0, step).start()
 
-        feats = jnp.dot(own, ob_v[1], preferred_element_type=jnp.float32) + jnp.dot(
-            middle, ob_v[0], preferred_element_type=jnp.float32)
+        feats = lax.dot_general(
+            own, ob_v[1], NT, preferred_element_type=jnp.float32
+        ) + lax.dot_general(middle, ob_v[0], NT, preferred_element_type=jnp.float32)
         example = se_ref[m * rows // (micro * rows // se_ref.shape[0])]
         lane_example = lax.rem(
             lax.broadcasted_iota(jnp.int32, feats.shape, 1) // rank_out, EXAMPLES)
@@ -170,8 +188,14 @@
     def lower(m):
         at = pl.ds(pl.multiple_of(m * rows, rows), rows)
         floats = buf_m[m, tp].astype(jnp.float32)
-        buf_l[m] = (floats + slope_of(h_ref[0, at, :]) * product(buf_m, m, 0)).astype(jnp.bfloat16)
-        for step in range(nz):
+        slope = slope_of(h_ref[0, at, :])
+        total = product(buf_m, m, 0, 0)
+        for ystep in range(1, ny):
+            for zstep in range(nz):
+                await_m(m, src_at(zstep, ystep))
+            total = product(buf_m, m, 0, ystep, total)
+        buf_l[m] = (floats + slope * total).astype(jnp.bfloat16)
+        for step in [*range(1, nz), 0]:
             lower_copy(m, step).start()
 
     def tp_copy(src, dst, ssem, rsem, to_tp):
@@ -195,14 +219,17 @@
                       score_recv.at[sec], to, tp)
 
     def project_inputs():
+        part_rows = part_in.shape[1]
+
         @pl.loop(0, tp_count)
         def _(k):
-            at = pl.ds(pl.multiple_of(k * rows, rows), rows)
+            at = pl.ds(pl.multiple_of(k * part_rows, part_rows), part_rows)
             total = None
             for layer in range(2):
                 floats = h_ref[layer, at, :].astype(jnp.float32)
                 activated = (floats * jax.nn.sigmoid(floats)).astype(jnp.bfloat16)
-                term = jnp.dot(activated, ib_v[layer], preferred_element_type=jnp.float32)
+                term = lax.dot_general(
+                    activated, ib_v[layer], NT, preferred_element_type=jnp.float32)
                 total = term if total is None else total + term
             part_in[k] = total
 
@@ -217,7 +244,7 @@
         for step in range(1, tp_count):
             full_copy(step).start()
 
-    @pl.when(jnp.logical_not(is_top))
+    @pl.when(sec < sections // 2)
     def _():
         project_inputs()
 
@@ -227,9 +254,12 @@
             for ystep in range(1, ny):
                 relay_m_copy(m, zstep, ystep).start()
 
-    @pl.loop(0, micro + 1)
+    @pl.loop(0, micro + 2)
     def _(it):
-        with_middle = jnp.logical_and(it >= 1, has_lower)
+        with_middle = jnp.logical_and(jnp.logical_and(it >= 1, it <= micro), has_lower)
+        lag = is_top.astype(jnp.int32)
+        m_low = it - 1 - lag
+        with_lower = jnp.logical_and(jnp.logical_and(m_low >= 0, m_low < micro), has_lower)
 
         @pl.when(jnp.logical_and(it < micro, jnp.logical_not(is_top)))
         def _():
@@ -257,28 +287,17 @@
                 for k in range(tp_count):
                     top_copy(it, k).wait()
 
-            @pl.when(jnp.logical_not(is_top))
-            def _():
-                for zstep in range(nz):
-                    for ystep in range(1, ny):
-                        await_u(it, src_at(zstep, ystep))
-
             upper(it)
 
-        @pl.when(with_middle)
-        def _():
-            m = it - 1
-
-            @pl.when(is_top)
-            def _():
-                pass_middle(m)
-
-            for zstep in range(nz):
-                for ystep in range(1, ny):
-                    await_m(m, src_at(zstep, ystep))
-            lower(m)
-
-    @pl.when(is_top)
+        @pl.when(jnp.logical_and(with_middle, is_top))
+        def _():
+            pass_middle(it - 1)
+
+        @pl.when(with_lower)
+        def _():
+            lower(m_low)
+
+    @pl.when(sec >= sections // 2)
     def _():
         project_inputs()
 
@@ -380,12 +399,12 @@
             pltpu.VMEM((micro, tp_count, rows, width), jnp.bfloat16),
             pltpu.VMEM((micro, rows, width), jnp.bfloat16),
             pltpu.VMEM(weights.shape, jnp.bfloat16),
-            pltpu.VMEM((2, width, 2 * pairs), jnp.bfloat16),
-            pltpu.VMEM((2, width, lanes), jnp.bfloat16),
+            pltpu.VMEM((2, 2 * pairs, width), jnp.bfloat16),
+            pltpu.VMEM((2, lanes, width), jnp.bfloat16),
             pltpu.VMEM((tokens, 2 * pairs), jnp.float32),
-            pltpu.VMEM((tp_count, rows, lanes), jnp.float32),
-            pltpu.VMEM((tp_count, rows, lanes), jnp.float32),
-            pltpu.VMEM((tp_count, rows, lanes), jnp.float32),
+            pltpu.VMEM((tp_count, tokens // tp_count, lanes), jnp.float32),
+            pltpu.VMEM((tp_count, tokens // tp_count, lanes), jnp.float32),
+            pltpu.VMEM((tp_count, tokens // tp_count, lanes), jnp.float32),
             pltpu.VMEM((tp_count, pairs, lanes), jnp.float32),
             pltpu.VMEM((pairs, lanes), jnp.float32),
             pltpu.VMEM((sections, 8, EXAMPLES * number), jnp.float32),
@@ -408,7 +427,9 @@
         ],
         compiler_params=pltpu.CompilerParams(
             collective_id=0, has_side_effects=True, vmem_limit_bytes=56 * 2**20),
-    )(top_cotangent, weights, layer_inputs, input_basis, output_basis, queries, sequence_example)
+    )(
+        top_cotangent, weights, layer_inputs, jnp.swapaxes(input_basis, 1, 2),
+        jnp.swapaxes(output_basis, 1, 2), queries, sequence_example)
 
 
 def solution(mesh):

time: 186 us -> 167 us (0.90)
  Pallas kernels: 181 us -> 166 us
  local copies, waits for them, and re-layouts: 4.65 us -> 1.24 us
    pallas_call x1, Pallas kernels: 181 us -> 166 us  [shards(): pl.pallas_call(functools.partial(chain_kernel, sections, tp_count), out_s...]
    unnamed x3 -> x1, local copies, waits for them, and re-layouts: 4.65 us -> 1.24 us
where the time goes in v3:
time: 167 us
  Pallas kernels  166 us (99%)
    pallas_call x1, Pallas kernels, shards(): pl.pallas_call(functools.partial(chain_kernel, sections, tp_count), out_s...  166 us

profile of v3, /device:TPU:0, one launch (start us, length us, event | category | flops | bytes accessed | tf_op | source)
XLA Modules:
  0.0 167.1 jit_solution(7283901439235900436)
XLA Ops:
  0.0 165.9 %shard_map.73 = f32[2,64]{1,0:T(2,128)} custom-call(bf16[512,4096]{1,0:T(8,128)(2,1)} %top_ref.1, bf16[2,512,4096]{2,1,0:T(8,128)(2,1)} %w_ref.1, bf16[2,512,512]{2,1,0:T(8,128)(2,1)} %h_ref.1, bf16[2,64,512]{2,1,0:T(8,128)(2,1)} %bitcast.2, bf16[2,32,512]{2,1,0:T(8,128)(2,1)} %bitcast.3, bf16[2,64,2048]{2,1,0:T(8,128)(2,1)} %q_ref.1, s32[4]{0:T(128)} %se_ref.1), custom_call_target="tpu_custom_call" | custom-call | tf_op jit(solution)/shard_map/pallas_call | solution.py:392
  165.9 1.2 copy.9

commit v4 on v3

--- a/solution.py
+++ b/solution.py
@@ -8,6 +8,7 @@
 from jax.sharding import PartitionSpec as P
 
 EXAMPLES = 2
+AHEAD = 4
 MESH = pl.DeviceIdType.MESH
 NT = (((1,), (1,)), ((), ()))
 
@@ -29,7 +30,7 @@
     sections, tp_count, top_ref, w_ref, h_ref, ib_ref, ob_ref, q_ref, se_ref, score_ref,
     buf_u, buf_m, buf_l, w_v, ob_v, ib_v, out_v, part_in, got_in, full_in, grad_v, sum_v, score_v,
     w_sem, recv_u, recv_m, send_m, send_my, relay_u, relay_m, send_l,
-    part_send, part_recv, full_send, full_recv, grad_send, grad_recv, score_send, score_recv,
+    part_send, part_recv, full_send, full_recv, grad_send, grad_recv, score_send, score_recv, credit,
 ):
     nz, ny = grid_of(tp_count)
     sec = lax.axis_index("section")
@@ -287,7 +288,16 @@
                 for k in range(tp_count):
                     top_copy(it, k).wait()
 
+            @pl.when(jnp.logical_and(is_top, it >= AHEAD))
+            def _():
+                pl.semaphore_wait(credit, 1)
+
             upper(it)
+
+            @pl.when(sec == sections - 2)
+            def _():
+                pl.semaphore_signal(
+                    credit, inc=1, device_id=(sec + 1, tp), device_id_type=MESH)
 
         @pl.when(jnp.logical_and(with_middle, is_top))
         def _():
@@ -348,6 +358,10 @@
     for example in range(EXAMPLES):
         score_ref[example:example + 1, :] = total[0:1, example * number:(example + 1) * number]
 
+    @pl.when(is_top)
+    def _():
+        pl.semaphore_wait(credit, min(AHEAD, micro))
+
     for step in range(1, tp_count):
         part_copy(step).wait_send()
         full_copy(step).wait_send()
@@ -424,6 +438,7 @@
             dma((tp_count,)),
             dma((sections,)),
             dma((sections,)),
+            pltpu.SemaphoreType.REGULAR,
         ],
         compiler_params=pltpu.CompilerParams(
             collective_id=0, has_side_effects=True, vmem_limit_bytes=56 * 2**20),

time: 167 us -> 165 us (0.988)
  Pallas kernels: 166 us -> 164 us
    pallas_call x1, Pallas kernels: 166 us -> 164 us  [shards(): pl.pallas_call(functools.partial(chain_kernel, sections, tp_count), out_s...]
where the time goes in v4:
time: 165 us
  Pallas kernels  164 us (99%)
    pallas_call x1, Pallas kernels, shards(): pl.pallas_call(functools.partial(chain_kernel, sections, tp_count), out_s...  164 us

profile of v4, /device:TPU:0, one launch (start us, length us, event | category | flops | bytes accessed | tf_op | source)
XLA Modules:
  0.0 165.0 jit_solution(2149510607902695910)
XLA Ops:
  0.0 163.8 %shard_map.73 = f32[2,64]{1,0:T(2,128)} custom-call(bf16[512,4096]{1,0:T(8,128)(2,1)} %top_ref.1, bf16[2,512,4096]{2,1,0:T(8,128)(2,1)} %w_ref.1, bf16[2,512,512]{2,1,0:T(8,128)(2,1)} %h_ref.1, bf16[2,64,512]{2,1,0:T(8,128)(2,1)} %bitcast.2, bf16[2,32,512]{2,1,0:T(8,128)(2,1)} %bitcast.3, bf16[2,64,2048]{2,1,0:T(8,128)(2,1)} %q_ref.1, s32[4]{0:T(128)} %se_ref.1), custom_call_target="tpu_custom_call" | custom-call | tf_op jit(solution)/shard_map/pallas_call | solution.py:406
  163.8 1.2 copy.9
